TPU v7x, 256 devices: a whole 4x4x8 slice. The times are simulated.
256 devices in a mesh: outer: 8 (over z), inner: 32 (over y, x, core).
Axes of the slice: x: 4, y: 4, z: 8, core: 2. Of those that a mesh axis runs over, the one named last changes fastest.
Arguments:
- queries: bfloat16 [262144, 1024], P(('outer', 'inner')), may hold values from -6 to 6
- keys: bfloat16 [262144, 1024], P(('outer', 'inner')), may hold values from -0.5 to 0.5
- values: bfloat16 [262144, 1024], P(('outer', 'inner')), may hold values from -6 to 6
- level_weights: float32 [19, 8, 262144], P(None, None, ('outer', 'inner')), as said below
- out_weight: bfloat16 [1024, 1024], replicated, may hold values from -0.046875 to 0.046875
Outputs:
- mixed: bfloat16 [262144, 1024], P(('outer', 'inner'))
Inputs may be any that keep to these rules, and one draw needn't show every extreme that they name: `level_weights`: every entry is positive.
All inputs are finite; a program needn't handle non-finite values.
Results may differ from a plain program's by a relative error of at most 0.0057.
Values sent between devices are 32-bit elements; how exact they have to be, the bound alone decides.
A program may use at most 128 MiB of HBM per device.

v0:
```python
import functools

import jax
import jax.numpy as jnp
from jax import lax
from jax.experimental import pallas as pl
from jax.experimental.pallas import tpu as pltpu
from jax.sharding import PartitionSpec as P

HEADS = 8
HEAD = 128
LOCAL_BITS = 10
TOK = 1024
TILE = 256
ITEMS = 8
ROWS = 64
MESH = pl.DeviceIdType.MESH
F32 = jnp.float32
BF16 = jnp.bfloat16

AT_C = 1
AT_X = 4
AT_Y = 7
AT_F1 = 9
AT_Z1 = 9
AT_Z2 = 11
AT_Z3 = 13
AT_F2 = 14
AT_L = 2
AT_R = 11
STEPS = ITEMS + AT_F2


def nt(a, b):
    return lax.dot_general(a, b, (((1,), (1,)), ((), ())), preferred_element_type=F32)


def nn(a, b):
    return jnp.dot(a, b, preferred_element_type=F32)


def bit_length(values, bits):
    count = jnp.zeros(values.shape, jnp.int32)
    for shift in range(bits):
        count = count + (jnp.right_shift(values, shift) > 0).astype(jnp.int32)
    return count


def diagonal_mixing(lam):
    group = lax.broadcasted_iota(jnp.int32, (16, 128), 0)
    token16 = lax.broadcasted_iota(jnp.int32, (16, 128), 1)
    far = bit_length(jnp.bitwise_xor(group, jnp.right_shift(token16, 3)), 4)
    coarse = jnp.where(far == 1, lam[4], jnp.where(far == 2, lam[5], jnp.where(far == 3, lam[6], lam[7])))
    coarse = jnp.where(group < jnp.right_shift(token16, 3), coarse, 0.0)
    row = lax.broadcasted_iota(jnp.int32, (8, 128), 0)
    token8 = jnp.bitwise_and(lax.broadcasted_iota(jnp.int32, (8, 128), 1), 7)
    near = bit_length(jnp.bitwise_xor(row, token8), 3)
    fine = jnp.where(near == 0, lam[0], jnp.where(near == 1, lam[1], jnp.where(near == 2, lam[2], lam[3])))
    fine = jnp.where(row <= token8, fine, 0.0)
    major = lax.broadcasted_iota(jnp.int32, (16, 8, 128), 0)
    token = lax.broadcasted_iota(jnp.int32, (16, 8, 128), 2)
    spread = jnp.broadcast_to(coarse[:, None, :], (16, 8, 128))
    return jnp.where(jnp.right_shift(token, 3) == major, fine[None], spread).reshape(128, 128)


def kernel(
    q_hbm, k_hbm, v_hbm, lam_hbm, out_hbm,
    qv, kv, vv, lamv, vt, st, ps, xb, sx, yb, sy, zo, z1b, z2b, z3b, p_out, q_out, fwd, bk, lst, acc, att,
    load_sem, core_s, core_r, x_s, x_r, y_s, y_r, z1_s, z1_r, z2_s, z2_r, z3_s, z3_r, f_s, f_r, out_sem,
):
    z = lax.axis_index("outer")
    inner = lax.axis_index("inner")
    c = inner % 2
    x = (inner // 2) % 4
    y = inner // 8

    def device(z_to, y_to, x_to, c_to):
        return (z_to, (y_to * 4 + x_to) * 2 + c_to)

    mate = device(z, y, x, 1 - c)

    def load(kind, h):
        cols = pl.ds(h * HEAD, HEAD)
        source, target = ((k_hbm, kv), (v_hbm, vv), (q_hbm, qv))[kind]
        return pltpu.make_async_copy(source.at[:, cols], target.at[h], load_sem.at[kind, h])

    def load_dyn(kind, h):
        target = (kv, vv, qv)[kind]
        return pltpu.make_async_copy(
            k_hbm.at[:, pl.ds(0, HEAD)], target.at[h], load_sem.at[kind, h])

    def lam_copy():
        return pltpu.make_async_copy(lam_hbm, lamv, load_sem.at[3, 0])

    for h in range(HEADS):
        load(0, h).start()
        load(1, h).start()
    lam_copy().start()
    for h in range(HEADS):
        load(2, h).start()

    barrier = pltpu.get_barrier_semaphore()
    peers = [mate]
    peers += [device(z, y, (x + d) % 4, c) for d in (1, 2, 3)]
    peers += [device(z, (y + d) % 4, x, c) for d in (1, 2, 3)]
    peers += [device((z + d) % 8, y, x, c) for d in range(1, 8)]
    for peer in peers:
        pl.semaphore_signal(barrier, inc=1, device_id=peer, device_id_type=MESH)

    def remote(src, dst, send, recv, to):
        return pltpu.make_async_remote_copy(
            src_ref=src, dst_ref=dst, send_sem=send, recv_sem=recv, device_id=to, device_id_type=MESH)

    def cp_core(h):
        return remote(st.at[h], ps.at[h], core_s.at[h], core_r.at[h], mate)

    def cp_x(i, d):
        return remote(xb.at[i, x], xb.at[i, x], x_s.at[i, d - 1], x_r.at[i, x], device(z, y, (x + d) % 4, c))

    def got_x(i, d):
        s = (x + d) % 4
        return remote(xb.at[i, s], xb.at[i, s], x_s.at[i, d - 1], x_r.at[i, s], device(z, y, s, c))

    def cp_y(i, d):
        return remote(yb.at[i, y], yb.at[i, y], y_s.at[i, d - 1], y_r.at[i, y], device(z, (y + d) % 4, x, c))

    def got_y(i, d):
        s = (y + d) % 4
        return remote(yb.at[i, s], yb.at[i, s], y_s.at[i, d - 1], y_r.at[i, s], device(z, s, x, c))

    def at_z(to):
        return device(to, y, x, c)

    z_pair = z + 1 - 2 * (z % 2)
    sends_1 = jnp.logical_or(z < 4, z % 2 == 0)
    gets_1 = jnp.logical_or(z < 4, z % 2 == 1)
    low = z % 4
    sends_2 = low == 1
    sends_2b = z == 2
    gets_2 = jnp.logical_or(low >= 2, z == 0)
    sends_3 = jnp.logical_or(z == 0, z == 3)
    gets_3 = z >= 4
    z3_a = jnp.where(z == 0, 7, 4)
    z3_b = jnp.where(z == 0, 6, 5)

    def cp_z1(i):
        return remote(zo.at[i], z1b.at[i], z1_s.at[i], z1_r.at[i], at_z(z_pair))

    def cp_z2(i, n, to):
        return remote(p_out.at[i], z2b.at[i], z2_s.at[i, n], z2_r.at[i], at_z(to))

    def cp_z3(i, n, to):
        return remote(q_out.at[i], z3b.at[i], z3_s.at[i, n], z3_r.at[i], at_z(to))

    def cp_f(src, i, n):
        return remote(src, fwd.at[i, n], f_s.at[i, n], f_r.at[i, n], mate)

    x_odd, x_high, y_odd, y_high = x % 2 == 1, x >= 2, y % 2 == 1, y >= 2
    z_odd, z_mid, z_high = z % 2 == 1, low >= 2, z >= 4
    has = (x_odd, x_high, y_odd, y_high, z_odd, z_mid, z_high)

    def fwd_source(i, n):
        return (
            lambda: xb.at[i, x - 1], lambda: sx.at[i], lambda: yb.at[i, y - 1], lambda: sy.at[i],
            lambda: z1b.at[i], lambda: z2b.at[i], lambda: z3b.at[i],
        )[n]()

    def hand_over(i, n):
        @pl.when(has[n])
        def _():
            source = fwd_source(i, n)
            cp_f(source, i, n).start()
            bk[2 * (i // 2) + c, 1 + n, i % 2] = source[...].astype(BF16)

    def take_over(i, n):
        @pl.when(has[n])
        def _():
            cp_f(fwd.at[i, n], i, n).wait_recv()
            bk[2 * (i // 2) + 1 - c, 1 + n, i % 2] = fwd[i, n].astype(BF16)

    def states(h):
        load_dyn(0, h).wait()
        load_dyn(1, h).wait()
        vt[h] = jnp.transpose(vv[h])
        part = []
        for p in range(4):
            part.append(nn(vt[h, :, p * TILE:(p + 1) * TILE], kv[h, p * TILE:(p + 1) * TILE, :]))
        first = part[0] + part[1]
        lst[h, 0] = part[0].astype(BF16)
        lst[h, 1] = part[2].astype(BF16)
        lst[h, 2] = first.astype(BF16)
        st[h] = (first + (part[2] + part[3])).reshape(2, ROWS, HEAD)

    def step_c(i):
        h = 2 * (i // 2) + c

        @pl.when(i % 2 == 0)
        def _():
            for n in range(2):
                cp_core(i + n).wait_recv()

                @pl.when(c == 1)
                def _():
                    bk[i + n, 0] = ps[i + n].astype(BF16)

        xb[i, x] = st[h, i % 2] + ps[h, i % 2]
        for d in (2, 1, 3):
            cp_x(i, d).start()

    def step_x(i):
        for d in (1, 2, 3):
            got_x(i, d).wait_recv()
        front = xb[i, 0] + xb[i, 1]
        sx[i] = front
        yb[i, y] = front + (xb[i, 2] + xb[i, 3])
        for d in (2, 1, 3):
            cp_y(i, d).start()
        hand_over(i, 0)
        hand_over(i, 1)

    def step_y(i):
        for d in (1, 2, 3):
            got_y(i, d).wait_recv()
        front = yb[i, 0] + yb[i, 1]
        sy[i] = front
        zo[i] = front + (yb[i, 2] + yb[i, 3])

        @pl.when(sends_1)
        def _():
            cp_z1(i).start()
        hand_over(i, 2)
        hand_over(i, 3)

    def step_z1(i):
        @pl.when(gets_1)
        def _():
            cp_z1(i).wait_recv()
            p_out[i] = zo[i] + z1b[i]

        @pl.when(sends_2)
        def _():
            cp_z2(i, 1, z + 2).start()
            cp_z2(i, 0, z + 1).start()

        @pl.when(sends_2b)
        def _():
            cp_z2(i, 0, 0).start()
        hand_over(i, 4)

    def step_z2(i):
        @pl.when(gets_2)
        def _():
            cp_z2(i, 0, 0).wait_recv()

        @pl.when(sends_3)
        def _():
            q_out[i] = p_out[i] + z2b[i]
            cp_z3(i, 1, z3_b).start()
            cp_z3(i, 0, z3_a).start()
        hand_over(i, 5)

    def step_z3(i):
        @pl.when(gets_3)
        def _():
            cp_z3(i, 0, 0).wait_recv()
        hand_over(i, 6)

    def local(h):
        load_dyn(2, h).wait()

        @pl.when(h == 0)
        def _():
            lam_copy().wait()
        for p in range(4):
            at = p * TILE
            qp = qv[h, at:at + TILE, :]
            kp = kv[h, at:at + TILE, :]
            scores = nt(kp, qp)
            rows = [lamv[l, pl.ds(h, 1), at:at + TILE] for l in range(LOCAL_BITS + 1)]
            mix_a = diagonal_mixing([row[:, :128] for row in rows[:8]])
            mix_b = diagonal_mixing([row[:, 128:] for row in rows[:8]])
            top = jnp.concatenate(
                [scores[:128, :128] * mix_a, scores[:128, 128:] * rows[8][:, 128:]], axis=1).astype(BF16)
            low_part = jnp.concatenate(
                [jnp.zeros((128, 128), BF16), (scores[128:, 128:] * mix_b).astype(BF16)], axis=1)
            weighted = jnp.concatenate([top, low_part], axis=0)
            total = nn(vt[h, :, at:at + TILE], weighted)
            if p % 2 == 1:
                total = total + rows[9] * nt(lst[h, p // 2], qp)
            if p >= 2:
                total = total + rows[10] * nt(lst[h, 2], qp)
            acc[h, :, at:at + TILE] = total

    def distant(h, first, last, done):
        count = last - first
        for p in range(4):
            at = p * TILE
            qp = qv[h, at:at + TILE, :]
            products = nt(bk[h, first:last].reshape(count * HEAD, HEAD), qp)
            total = acc[h, :, at:at + TILE]
            for n in range(count):
                row = lamv[LOCAL_BITS + 1 + first + n, pl.ds(h, 1), at:at + TILE]
                total = total + products[n * HEAD:(n + 1) * HEAD] * row
            if done:
                att[h, :, at:at + TILE] = total.astype(BF16)
            else:
                acc[h, :, at:at + TILE] = total

    def out_copy(h):
        return pltpu.make_async_copy(
            att.at[h], out_hbm.at[pl.ds(pl.multiple_of(h * HEAD, HEAD), HEAD), :], out_sem.at[h])

    def when_in(t, at, count):
        return jnp.logical_and(t >= at, t < at + count)

    def step(t, carry):
        def stage(at, run, count=ITEMS):
            @pl.when(when_in(t, at, count))
            def _():
                run(t - at)

        stage(AT_Z3, step_z3)
        stage(AT_Z2, step_z2)
        stage(AT_Z1, step_z1)
        stage(AT_Y, step_y)
        stage(AT_X, step_x)
        stage(AT_C, step_c)

        @pl.when(jnp.logical_and(jnp.logical_and(t % 2 == 0, t > 0), t < ITEMS))
        def _():
            for n in range(2):
                states(t + n)
                cp_core(t + n).start()

        stage(AT_L, local)

        def f1(i):
            for n in range(4):
                take_over(i, n)
        stage(AT_F1, f1)
        stage(AT_R, lambda h: distant(h, 0, 5, False))

        def f2(i):
            for n in range(4, 7):
                take_over(i, n)

            @pl.when(i % 2 == 1)
            def _():
                for n in range(2):
                    distant(i - 1 + n, 5, 8, True)
                    out_copy(i - 1 + n).start()
        stage(AT_F2, f2)
        return carry

    bk[...] = jnp.zeros(bk.shape, BF16)
    states(0)
    states(1)
    pl.semaphore_wait(barrier, len(peers))
    cp_core(0).start()
    cp_core(1).start()
    lax.fori_loop(1, STEPS, step, 0)

    def drain(i, carry):
        cp_core(i).wait_send()
        for d in (1, 2, 3):
            cp_x(i, d).wait_send()
            cp_y(i, d).wait_send()

        @pl.when(sends_1)
        def _():
            cp_z1(i).wait_send()

        @pl.when(jnp.logical_or(sends_2, sends_2b))
        def _():
            cp_z2(i, 0, 0).wait_send()

        @pl.when(sends_2)
        def _():
            cp_z2(i, 1, 0).wait_send()

        @pl.when(sends_3)
        def _():
            cp_z3(i, 0, 0).wait_send()
            cp_z3(i, 1, 0).wait_send()
        for n in range(7):
            @pl.when(has[n])
            def _():
                cp_f(fwd.at[i, n], i, n).wait_send()
        out_copy(i).wait()
        return carry

    lax.fori_loop(0, ITEMS, drain, 0)


def attend(queries, keys, values, level_weights):
    item = (ROWS, HEAD)
    dma = pltpu.SemaphoreType.DMA
    scratch = [
        pltpu.VMEM((HEADS, TOK, HEAD), BF16),
        pltpu.VMEM((HEADS, TOK, HEAD), BF16),
        pltpu.VMEM((HEADS, TOK, HEAD), BF16),
        pltpu.VMEM(level_weights.shape, F32),
        pltpu.VMEM((HEADS, HEAD, TOK), BF16),
        pltpu.VMEM((HEADS, 2) + item, F32),
        pltpu.VMEM((HEADS, 2) + item, F32),
        pltpu.VMEM((ITEMS, 4) + item, F32),
        pltpu.VMEM((ITEMS,) + item, F32),
        pltpu.VMEM((ITEMS, 4) + item, F32),
        pltpu.VMEM((ITEMS,) + item, F32),
        pltpu.VMEM((ITEMS,) + item, F32),
        pltpu.VMEM((ITEMS,) + item, F32),
        pltpu.VMEM((ITEMS,) + item, F32),
        pltpu.VMEM((ITEMS,) + item, F32),
        pltpu.VMEM((ITEMS,) + item, F32),
        pltpu.VMEM((ITEMS,) + item, F32),
        pltpu.VMEM((ITEMS, 7) + item, F32),
        pltpu.VMEM((HEADS, 8, 2) + item, BF16),
        pltpu.VMEM((HEADS, 3, HEAD, HEAD), BF16),
        pltpu.VMEM((HEADS, HEAD, TOK), F32),
        pltpu.VMEM((HEADS, HEAD, TOK), BF16),
        dma((4, HEADS)),
        dma((HEADS,)), dma((HEADS,)),
        dma((ITEMS, 3)), dma((ITEMS, 4)),
        dma((ITEMS, 3)), dma((ITEMS, 4)),
        dma((ITEMS,)), dma((ITEMS,)),
        dma((ITEMS, 2)), dma((ITEMS,)),
        dma((ITEMS, 2)), dma((ITEMS,)),
        dma((ITEMS, 7)), dma((ITEMS, 7)),
        dma((HEADS,)),
    ]
    return pl.pallas_call(
        kernel,
        out_shape=jax.ShapeDtypeStruct((HEADS * HEAD, TOK), BF16),
        in_specs=[pl.BlockSpec(memory_space=pl.ANY)] * 4,
        out_specs=pl.BlockSpec(memory_space=pl.ANY),
        scratch_shapes=scratch,
        compiler_params=pltpu.CompilerParams(
            collective_id=0, has_side_effects=True, vmem_limit_bytes=60 << 20),
    )(queries, keys, values, level_weights)


def body(queries, keys, values, level_weights, out_weight):
    attended = attend(queries, keys, values, level_weights)
    return lax.dot_general(
        attended, out_weight, (((0,), (0,)), ((), ())), preferred_element_type=F32).astype(BF16)


def solution(mesh):
    rows = P(("outer", "inner"), None)
    in_specs = (rows, rows, rows, P(None, None, ("outer", "inner")), P())
    return jax.shard_map(body, mesh=mesh, in_specs=in_specs, out_specs=rows, check_vma=False)
```

profile of v0, /device:TPU:193, one launch (start us, length us, event | category | flops | bytes accessed | tf_op | source)
XLA Modules:
  0.0 47.8 jit_solution(17924477349530854974)
XLA Ops:
  0.0 0.0 copy-start
  0.0 42.5 %shard_map.55 = bf16[1024,1024]{1,0:T(8,128)(2,1)} custom-call(bf16[1024,1024]{1,0:T(8,128)(2,1)} %q_hbm.1, bf16[1024,1024]{1,0:T(8,128)(2,1)} %k_hbm.1, bf16[1024,1024]{1,0:T(8,128)(2,1)} %v_hbm.1, f32[19,8,1024]{2,1,0:T(8,128)} %lam_hbm.1), custom_call_target="tpu_custom_call" | custom-call | tf_op jit(solution)/shard_map/pallas_call | solution.py:431
  42.5 0.0 copy-done
  42.5 5.3 %convolution_convert_fusion = bf16[1024,1024]{1,0:T(8,128)(2,1)} fusion(bf16[1024,1024]{1,0:T(8,128)(2,1)} %shard_map.55, bf16[1024,1024]{1,0:T(8,128)(2,1)S(1)} %copy-done), kind=kOutput, calls=%fused_computation | convolution fusion | flops 2148532224 | bytes 6291456 | tf_op jit(solution)/shard_map/dot_general | solution.py:444
Async XLA Ops:
  0.0 42.5 %copy-start = (bf16[1024,1024]{1,0:T(8,128)(2,1)S(1)}, bf16[1024,1024]{1,0:T(8,128)(2,1)}, u32[]{:S(2)}) copy-start(bf16[1024,1024]{1,0:T(8,128)(2,1)} %param.9) | copy-start | bytes 6291460
where the time goes:
time: 47.9 us; the launch traced here: 47.8 us
  Pallas kernels  42.5 us (89%)
  matrix products  5.3 us (11%)
    pallas_call x1, Pallas kernels, attend(): pl.pallas_call(kernel, out_shape=jax.ShapeDtypeStruct((HEADS * HEAD, TOK)...  42.5 us
    dot_general x1, matrix products, body(): lax.dot_general(attended, out_weight, (((0,), (0,)), ((), ())), preferred...  5.3 us

commit v1 on v0

v1 whole, which is shorter than its diff:
```python
import jax
import jax.numpy as jnp
from jax import lax
from jax.experimental import pallas as pl
from jax.experimental.pallas import tpu as pltpu
from jax.sharding import PartitionSpec as P

HEADS = 8
HEAD = 128
LOCAL_BITS = 10
TOK = 1024
TILE = 256
VMEM_MIB = 50
PARTS = 2
ITEMS = 4 * PARTS
ROWS = HEAD // PARTS
STRIDE = PARTS // 2
MESH = pl.DeviceIdType.MESH
F32 = jnp.float32
BF16 = jnp.bfloat16

AT_C = 1
AT_X = 4
AT_Y = 7
AT_F1 = 9
AT_Z1 = 9
AT_Z2 = 12
AT_Z3 = 15
AT_F2 = 16
AT_L = 3
AT_R = 13
STEPS = ITEMS + AT_F2


def nt(a, b):
    return lax.dot_general(a, b, (((1,), (1,)), ((), ())), preferred_element_type=F32)


def nn(a, b):
    return jnp.dot(a, b, preferred_element_type=F32)


def bit_length(values, bits):
    count = jnp.zeros(values.shape, jnp.int32)
    for shift in range(bits):
        count = count + (jnp.right_shift(values, shift) > 0).astype(jnp.int32)
    return count


def diagonal_mixing(lam):
    group = lax.broadcasted_iota(jnp.int32, (16, 128), 0)
    token16 = lax.broadcasted_iota(jnp.int32, (16, 128), 1)
    far = bit_length(jnp.bitwise_xor(group, jnp.right_shift(token16, 3)), 4)
    coarse = jnp.where(far == 1, lam[4], jnp.where(far == 2, lam[5], jnp.where(far == 3, lam[6], lam[7])))
    coarse = jnp.where(group < jnp.right_shift(token16, 3), coarse, 0.0)
    row = lax.broadcasted_iota(jnp.int32, (8, 128), 0)
    token8 = jnp.bitwise_and(lax.broadcasted_iota(jnp.int32, (8, 128), 1), 7)
    near = bit_length(jnp.bitwise_xor(row, token8), 3)
    fine = jnp.where(near == 0, lam[0], jnp.where(near == 1, lam[1], jnp.where(near == 2, lam[2], lam[3])))
    fine = jnp.where(row <= token8, fine, 0.0)
    major = lax.broadcasted_iota(jnp.int32, (16, 8, 128), 0)
    token = lax.broadcasted_iota(jnp.int32, (16, 8, 128), 2)
    spread = jnp.broadcast_to(coarse[:, None, :], (16, 8, 128))
    return jnp.where(jnp.right_shift(token, 3) == major, fine[None], spread).reshape(128, 128)


def kernel(
    q_hbm, k_hbm, v_hbm, lam_hbm, out_hbm,
    qv, kv, vv, lamv, vt, st, ps, xb, sx, yb, sy, zo, zr, p_out, q_out, fwd, bk, lst, acc, att_t, att,
    load_sem, whole_sem, core_s, core_r, x_s, x_r, y_s, y_r, z_s, z_r, f_s, f_r, out_sem,
):
    z = lax.axis_index("outer")
    inner = lax.axis_index("inner")
    c = inner % 2
    x = (inner // 2) % 4
    y = inner // 8

    def device(z_to, y_to, x_to, c_to):
        return (z_to, (y_to * 4 + x_to) * 2 + c_to)

    mate = device(z, y, x, 1 - c)

    def load(kind, h, source_h):
        source, target = ((k_hbm, kv), (v_hbm, vv), (q_hbm, qv))[kind]
        return pltpu.make_async_copy(
            source.at[:, pl.ds(source_h * HEAD, HEAD)], target.at[h], load_sem.at[kind, h])

    lam_copy = pltpu.make_async_copy(lam_hbm, lamv, whole_sem.at[0])

    for h in range(HEADS):
        load(0, h, h).start()
        load(1, h, h).start()
    lam_copy.start()
    for h in range(HEADS):
        load(2, h, h).start()

    barrier = pltpu.get_barrier_semaphore()
    peers = [mate]
    peers += [device(z, y, (x + d) % 4, c) for d in (1, 2, 3)]
    peers += [device(z, (y + d) % 4, x, c) for d in (1, 2, 3)]
    peers += [device((z + d) % 8, y, x, c) for d in (1, 7, 2, 6)]
    for peer in peers:
        pl.semaphore_signal(barrier, inc=1, device_id=peer, device_id_type=MESH)

    def remote(src, dst, send, recv, to):
        return pltpu.make_async_remote_copy(
            src_ref=src, dst_ref=dst, send_sem=send, recv_sem=recv, device_id=to, device_id_type=MESH)

    def at_x(d):
        return device(z, y, (x + d) % 4, c)

    def at_y(d):
        return device(z, (y + d) % 4, x, c)

    def at_z(to):
        return device(to, y, x, c)

    def cp_core(h):
        return remote(st.at[h], ps.at[h], core_s.at[0], core_r.at[h // 2], mate)

    def got_core(k):
        pair = ps.at[pl.ds(2 * k, 2)]
        return remote(pair, pair, core_s.at[0], core_r.at[k], mate)

    def cp_x(i, d):
        return remote(xb.at[i, x], xb.at[i, x], x_s.at[0], x_r.at[i], at_x(d))

    def got_x(i):
        return remote(xb.at[i, pl.ds(0, 3)], xb.at[i, pl.ds(0, 3)], x_s.at[0], x_r.at[i], at_x(1))

    def cp_y(i, d):
        return remote(yb.at[i, y], yb.at[i, y], y_s.at[0], y_r.at[i], at_y(d))

    def got_y(i):
        return remote(yb.at[i, pl.ds(0, 3)], yb.at[i, pl.ds(0, 3)], y_s.at[0], y_r.at[i], at_y(1))

    x_pair = x + 1 - 2 * (x % 2)
    y_pair = y + 1 - 2 * (y % 2)
    z_pair = z + 1 - 2 * (z % 2)
    low = z % 4
    sends_1 = jnp.logical_or(z < 4, z % 2 == 0)
    gets_1 = jnp.logical_or(z < 4, z % 2 == 1)
    sends_2 = low == 1
    sends_2b = z == 2
    gets_2 = jnp.logical_or(low >= 2, z == 0)
    sends_3 = jnp.logical_or(z == 0, z == 3)
    gets_3 = z >= 4
    z3_a = jnp.where(z == 0, 7, 4)
    z3_b = jnp.where(z == 0, 6, 5)

    def cp_z(n, source, i, to):
        return remote(source.at[i], zr.at[i, n], z_s.at[n], z_r.at[i, n], at_z(to))

    def got_z(n, i):
        return remote(zr.at[i, n], zr.at[i, n], z_s.at[n], z_r.at[i, n], at_z(z_pair))

    def sent_z(n, source):
        return remote(source, source, z_s.at[n], z_r.at[0, n], at_z(z_pair))

    has = (x % 2 == 1, x >= 2, y % 2 == 1, y >= 2, z % 2 == 1, low >= 2, z >= 4)
    places = ((0, 2), (2, 2), (4, 3))

    def cp_f(source, i, kind):
        first, count = places[kind]
        return remote(source.at[i], fwd.at[i, pl.ds(first, count)], f_s.at[0], f_r.at[i, kind], mate)

    def keep(h, i, n, value):
        bk[h, 1 + n, i % PARTS] = jnp.where(has[n], value, 0.0).astype(BF16)

    def hand_over(source, i, kind):
        cp_f(source, i, kind).start()
        first, count = places[kind]
        for n in range(count):
            keep(2 * (i // PARTS) + c, i, first + n, source[i, n])

    def take_over(i, kind):
        first, count = places[kind]
        there = fwd.at[i, pl.ds(first, count)]
        remote(there, there, f_s.at[0], f_r.at[i, kind], mate).wait_recv()
        for n in range(count):
            keep(2 * (i // PARTS) + 1 - c, i, first + n, fwd[i, first + n])

    def states(h):
        load(0, h, 0).wait()
        load(1, h, 0).wait()
        vt[h] = jnp.transpose(vv[h])
        part = []
        for p in range(4):
            part.append(nn(vt[h, :, p * TILE:(p + 1) * TILE], kv[h, p * TILE:(p + 1) * TILE, :]))
        first = part[0] + part[1]
        lst[h, 0] = part[0].astype(BF16)
        lst[h, 1] = part[2].astype(BF16)
        lst[h, 2] = first.astype(BF16)
        st[h] = (first + (part[2] + part[3])).reshape(PARTS, ROWS, HEAD)

    def step_c(i):
        h = 2 * (i // PARTS) + c

        @pl.when(i % PARTS == 0)
        def _():
            got_core(i // PARTS).wait_recv()
            for n in range(2):
                g = 2 * (i // PARTS) + n
                bk[g, 0] = jnp.where(c == 1, ps[g], 0.0).astype(BF16)

        xb[i, x] = st[h, i % PARTS] + ps[h, i % PARTS]
        for d in (2, 1, 3):
            cp_x(i, d).start()

    def step_x(i):
        got_x(i).wait_recv()
        front = xb[i, 0] + xb[i, 1]
        yb[i, y] = front + (xb[i, 2] + xb[i, 3])
        for d in (2, 1, 3):
            cp_y(i, d).start()
        sx[i, 0] = xb[i, x_pair]
        sx[i, 1] = front
        hand_over(sx, i, 0)

    def step_y(i):
        got_y(i).wait_recv()
        front = yb[i, 0] + yb[i, 1]
        zo[i] = front + (yb[i, 2] + yb[i, 3])

        @pl.when(sends_1)
        def _():
            cp_z(0, zo, i, z_pair).start()
        sy[i, 0] = yb[i, y_pair]
        sy[i, 1] = front
        hand_over(sy, i, 1)

    def step_z1(i):
        @pl.when(gets_1)
        def _():
            got_z(0, i).wait_recv()
            p_out[i] = zo[i] + zr[i, 0]

        @pl.when(sends_2)
        def _():
            cp_z(1, p_out, i, z + 2).start()
            cp_z(1, p_out, i, z + 1).start()

        @pl.when(sends_2b)
        def _():
            cp_z(1, p_out, i, 0).start()

    def step_z2(i):
        @pl.when(gets_2)
        def _():
            got_z(1, i).wait_recv()

        @pl.when(sends_3)
        def _():
            q_out[i] = p_out[i] + zr[i, 1]
            cp_z(2, q_out, i, z3_b).start()
            cp_z(2, q_out, i, z3_a).start()

    def step_z3(i):
        @pl.when(gets_3)
        def _():
            got_z(2, i).wait_recv()
        hand_over(zr, i, 2)

    def local(h):
        load(2, h, 0).wait()

        @pl.when(h == 0)
        def _():
            lam_copy.wait()
        for p in range(4):
            at = p * TILE
            qp = qv[h, at:at + TILE, :]
            kp = kv[h, at:at + TILE, :]
            scores = nt(kp, qp)
            rows = [lamv[l, pl.ds(h, 1), at:at + TILE] for l in range(LOCAL_BITS + 1)]
            mix_a = diagonal_mixing([row[:, :128] for row in rows[:8]])
            mix_b = diagonal_mixing([row[:, 128:] for row in rows[:8]])
            top = jnp.concatenate(
                [scores[:128, :128] * mix_a, scores[:128, 128:] * rows[8][:, 128:]], axis=1).astype(BF16)
            low_part = jnp.concatenate(
                [jnp.zeros((128, 128), BF16), (scores[128:, 128:] * mix_b).astype(BF16)], axis=1)
            weighted = jnp.concatenate([top, low_part], axis=0)
            total = nn(vt[h, :, at:at + TILE], weighted)
            if p % 2 == 1:
                total = total + rows[9] * nt(lst[h, p // 2], qp)
            if p >= 2:
                total = total + rows[10] * nt(lst[h, 2], qp)
            acc[h, :, :, at:at + TILE] = total.reshape(PARTS, ROWS, TILE)

    def distant(states_there, h, p, first, total):
        at = p * TILE
        rows = total.shape[0]
        products = nt(states_there, qv[h, at:at + TILE, :])
        for n in range(states_there.shape[0] // rows):
            row = lamv[LOCAL_BITS + 1 + first + n, pl.ds(h, 1), at:at + TILE]
            total = total + products[n * rows:(n + 1) * rows] * row
        return total

    def near_buckets(h):
        for p in range(4):
            at = p * TILE
            total = distant(bk[h, 0:5].reshape(5 * HEAD, HEAD), h, p, 0, acc[h, :, :, at:at + TILE].reshape(HEAD, TILE))
            acc[h, :, :, at:at + TILE] = total.reshape(PARTS, ROWS, TILE)

    def out_copy(h):
        return pltpu.make_async_copy(
            att.at[h], out_hbm.at[:, pl.ds(pl.multiple_of(h * HEAD, HEAD), HEAD)], out_sem.at[h])

    def far_buckets(i):
        part = i % PARTS
        for n in range(2):
            h = 2 * (i // PARTS) + n
            for p in range(4):
                at = p * TILE
                total = distant(bk[h, 5:8, part].reshape(3 * ROWS, HEAD), h, p, 5, acc[h, part, :, at:at + TILE])
                att_t[h, part, :, at:at + TILE] = total.astype(BF16)

        @pl.when(part == PARTS - 1)
        def _():
            for n in range(2):
                h = 2 * (i // PARTS) + n
                att[h] = jnp.transpose(att_t[h].reshape(HEAD, TOK))
                out_copy(h).start()

    def when_in(t, at, count):
        return jnp.logical_and(t >= at, t < at + count)

    def step(t, carry):
        def stage(at, run, count=ITEMS):
            @pl.when(when_in(t, at, count))
            def _():
                run(t - at)

        def spread(at, run):
            @pl.when(jnp.logical_and(when_in(t, at, HEADS * STRIDE), (t - at) % STRIDE == 0))
            def _():
                run((t - at) // STRIDE)

        def f1(i):
            take_over(i, 0)
            take_over(i, 1)

        def f2(i):
            take_over(i, 2)
            far_buckets(i)

        stage(AT_X, step_x)
        stage(AT_Z3, step_z3)
        stage(AT_Z2, step_z2)
        stage(AT_Y, step_y)
        stage(AT_Z1, step_z1)
        stage(AT_C, step_c)

        @pl.when(jnp.logical_and(t % PARTS == 0, t < ITEMS))
        def _():
            for n in range(2):
                g = 2 * (t // PARTS) + n
                states(g)
                cp_core(g).start()

        stage(AT_F1, f1)
        stage(AT_F2, f2)
        early = jnp.logical_and(jnp.logical_and(t >= AT_L, t < AT_L + 6), (t - AT_L) % 2 == 0)
        late = when_in(t, AT_L + 5, HEADS - 3)

        @pl.when(jnp.logical_or(early, late))
        def _():
            local(jnp.where(early, (t - AT_L) // 2, t - AT_L - 2))
        spread(AT_R, near_buckets)
        return carry

    states(0)
    states(1)
    pl.semaphore_wait(barrier, len(peers))
    cp_core(0).start()
    cp_core(1).start()
    lax.fori_loop(1, STEPS, step, 0)

    remote(st, st, core_s.at[0], core_r.at[0], mate).wait_send()
    remote(xb.at[:, pl.ds(0, 3)], xb.at[:, pl.ds(0, 3)], x_s.at[0], x_r.at[0], at_x(1)).wait_send()
    remote(yb.at[:, pl.ds(0, 3)], yb.at[:, pl.ds(0, 3)], y_s.at[0], y_r.at[0], at_y(1)).wait_send()

    @pl.when(sends_1)
    def _():
        sent_z(0, zo).wait_send()

    @pl.when(sends_2)
    def _():
        sent_z(1, sx).wait_send()

    @pl.when(sends_2b)
    def _():
        sent_z(1, zo).wait_send()

    @pl.when(sends_3)
    def _():
        sent_z(2, sx).wait_send()
    remote(fwd, fwd, f_s.at[0], f_r.at[0, 0], mate).wait_send()
    for h in range(HEADS):
        out_copy(h).wait()


def layer(queries, keys, values, level_weights, out_weight):
    item = (ROWS, HEAD)
    dma = pltpu.SemaphoreType.DMA
    scratch = [
        pltpu.VMEM((HEADS, TOK, HEAD), BF16),
        pltpu.VMEM((HEADS, TOK, HEAD), BF16),
        pltpu.VMEM((HEADS, TOK, HEAD), BF16),
        pltpu.VMEM(level_weights.shape, F32),
        pltpu.VMEM((HEADS, HEAD, TOK), BF16),
        pltpu.VMEM((HEADS, PARTS) + item, F32),
        pltpu.VMEM((HEADS, PARTS) + item, F32),
        pltpu.VMEM((ITEMS, 4) + item, F32),
        pltpu.VMEM((ITEMS, 2) + item, F32),
        pltpu.VMEM((ITEMS, 4) + item, F32),
        pltpu.VMEM((ITEMS, 2) + item, F32),
        pltpu.VMEM((ITEMS,) + item, F32),
        pltpu.VMEM((ITEMS, 3) + item, F32),
        pltpu.VMEM((ITEMS,) + item, F32),
        pltpu.VMEM((ITEMS,) + item, F32),
        pltpu.VMEM((ITEMS, 7) + item, F32),
        pltpu.VMEM((HEADS, 8, PARTS) + item, BF16),
        pltpu.VMEM((HEADS, 3, HEAD, HEAD), BF16),
        pltpu.VMEM((HEADS, PARTS, ROWS, TOK), F32),
        pltpu.VMEM((HEADS, PARTS, ROWS, TOK), BF16),
        pltpu.VMEM((HEADS, TOK, HEAD), BF16),
        dma((3, HEADS)), dma((1,)),
        dma((1,)), dma((HEADS // 2,)),
        dma((1,)), dma((ITEMS,)),
        dma((1,)), dma((ITEMS,)),
        dma((3,)), dma((ITEMS, 3)),
        dma((1,)), dma((ITEMS, 3)),
        dma((HEADS,)),
    ]
    attended = pl.pallas_call(
        kernel,
        out_shape=jax.ShapeDtypeStruct((TOK, HEADS * HEAD), BF16),
        in_specs=[pl.BlockSpec(memory_space=pl.ANY)] * 4,
        out_specs=pl.BlockSpec(memory_space=pl.ANY),
        scratch_shapes=scratch,
        compiler_params=pltpu.CompilerParams(
            collective_id=0, has_side_effects=True, vmem_limit_bytes=VMEM_MIB << 20),
    )(*[pltpu.with_memory_space_constraint(a, pltpu.HBM) for a in (queries, keys, values, level_weights)])
    return jnp.dot(attended, out_weight, preferred_element_type=F32).astype(BF16)


def solution(mesh):
    rows = P(("outer", "inner"), None)
    in_specs = (rows, rows, rows, P(None, None, ("outer", "inner")), P())
    return jax.shard_map(layer, mesh=mesh, in_specs=in_specs, out_specs=rows, check_vma=False)
```

time: 47.9 us -> 45.5 us (0.950)
  the two profiles are of different devices: /device:TPU:193 before, /device:TPU:1 now
where the time goes in v1:
time: 45.5 us
  Pallas kernels  41.8 us (92%)
  matrix products  3.65 us (8%)
    pallas_call x1, Pallas kernels, layer(): pl.pallas_call(kernel, out_shape=jax.ShapeDtypeStruct((TOK, HEADS * HEAD)...  41.8 us
    dot_general x1, matrix products, layer(): jnp.dot(attended, out_weight, preferred_element_type=F32).astype(BF16)  3.65 us

profile of v1, /device:TPU:1, one launch (start us, length us, event | category | flops | bytes accessed | tf_op | source)
XLA Modules:
  0.0 45.5 jit_solution(6167215540679775101)
XLA Ops:
  0.0 0.0 copy-start
  0.0 41.8 %shard_map.55 = bf16[1024,1024]{1,0:T(8,128)(2,1)S(1)} custom-call(bf16[1024,1024]{1,0:T(8,128)(2,1)} %q_hbm.1, bf16[1024,1024]{1,0:T(8,128)(2,1)} %k_hbm.1, bf16[1024,1024]{1,0:T(8,128)(2,1)} %v_hbm.1, f32[19,8,1024]{2,1,0:T(8,128)} %lam_hbm.1), custom_call_target="tpu_custom_call" | custom-call | tf_op jit(solution)/shard_map/pallas_call | solution.py:436
  41.8 0.0 copy-done
  41.8 3.7 %convolution_convert_fusion = bf16[1024,1024]{1,0:T(8,128)(2,1)} fusion(bf16[1024,1024]{1,0:T(8,128)(2,1)S(1)} %shard_map.55, bf16[1024,1024]{1,0:T(8,128)(2,1)S(1)} %copy-done), kind=kOutput, calls=%fused_computation | convolution fusion | flops 2148532224 | bytes 6291456 | tf_op jit(solution)/shard_map/dot_general | solution.py:445
Async XLA Ops:
  0.0 41.8 %copy-start = (bf16[1024,1024]{1,0:T(8,128)(2,1)S(1)}, bf16[1024,1024]{1,0:T(8,128)(2,1)}, u32[]{:S(2)}) copy-start(bf16[1024,1024]{1,0:T(8,128)(2,1)} %param.9) | copy-start | bytes 6291460

commit v2 on v1

--- a/solution.py
+++ b/solution.py
@@ -65,9 +65,9 @@
 
 
 def kernel(
-    q_hbm, k_hbm, v_hbm, lam_hbm, out_hbm,
-    qv, kv, vv, lamv, vt, st, ps, xb, sx, yb, sy, zo, zr, p_out, q_out, fwd, bk, lst, acc, att_t, att,
-    load_sem, whole_sem, core_s, core_r, x_s, x_r, y_s, y_r, z_s, z_r, f_s, f_r, out_sem,
+    q_hbm, k_hbm, v_hbm, lam_hbm, out,
+    qv, kv, vv, lamv, vt, st, ps, xb, sx, yb, sy, zo, zr, p_out, q_out, fwd, bk, lst, acc,
+    load_sem, whole_sem, core_s, core_r, x_s, x_r, y_s, y_r, z_s, z_r, f_s, f_r,
 ):
     z = lax.axis_index("outer")
     inner = lax.axis_index("inner")
@@ -267,60 +267,50 @@
         @pl.when(h == 0)
         def _():
             lam_copy.wait()
+        queries = [qv[h, p * TILE:(p + 1) * TILE, :] for p in range(4)]
+        scores = [nt(kv[h, p * TILE:(p + 1) * TILE, :], queries[p]) for p in range(4)]
+        blocks = {p: nt(lst[h, n], queries[p]) for n, p in enumerate((1, 3))}
+        halves = {p: nt(lst[h, 2], queries[p]) for p in (2, 3)}
         for p in range(4):
             at = p * TILE
-            qp = qv[h, at:at + TILE, :]
-            kp = kv[h, at:at + TILE, :]
-            scores = nt(kp, qp)
+            score = scores[p]
             rows = [lamv[l, pl.ds(h, 1), at:at + TILE] for l in range(LOCAL_BITS + 1)]
             mix_a = diagonal_mixing([row[:, :128] for row in rows[:8]])
             mix_b = diagonal_mixing([row[:, 128:] for row in rows[:8]])
             top = jnp.concatenate(
-                [scores[:128, :128] * mix_a, scores[:128, 128:] * rows[8][:, 128:]], axis=1).astype(BF16)
+                [score[:128, :128] * mix_a, score[:128, 128:] * rows[8][:, 128:]], axis=1).astype(BF16)
             low_part = jnp.concatenate(
-                [jnp.zeros((128, 128), BF16), (scores[128:, 128:] * mix_b).astype(BF16)], axis=1)
+                [jnp.zeros((128, 128), BF16), (score[128:, 128:] * mix_b).astype(BF16)], axis=1)
             weighted = jnp.concatenate([top, low_part], axis=0)
             total = nn(vt[h, :, at:at + TILE], weighted)
-            if p % 2 == 1:
-                total = total + rows[9] * nt(lst[h, p // 2], qp)
-            if p >= 2:
-                total = total + rows[10] * nt(lst[h, 2], qp)
+            if p in blocks:
+                total = total + rows[9] * blocks[p]
+            if p in halves:
+                total = total + rows[10] * halves[p]
             acc[h, :, :, at:at + TILE] = total.reshape(PARTS, ROWS, TILE)
 
-    def distant(states_there, h, p, first, total):
-        at = p * TILE
-        rows = total.shape[0]
-        products = nt(states_there, qv[h, at:at + TILE, :])
-        for n in range(states_there.shape[0] // rows):
-            row = lamv[LOCAL_BITS + 1 + first + n, pl.ds(h, 1), at:at + TILE]
-            total = total + products[n * rows:(n + 1) * rows] * row
-        return total
+    def distant(states_there, h, first, totals):
+        rows = totals[0].shape[0]
+        products = [nt(states_there, qv[h, p * TILE:(p + 1) * TILE, :]) for p in range(4)]
+        for p in range(4):
+            total = totals[p]
+            for n in range(states_there.shape[0] // rows):
+                row = lamv[LOCAL_BITS + 1 + first + n, pl.ds(h, 1), p * TILE:(p + 1) * TILE]
+                total = total + products[p][n * rows:(n + 1) * rows] * row
+            yield p, total
 
     def near_buckets(h):
-        for p in range(4):
-            at = p * TILE
-            total = distant(bk[h, 0:5].reshape(5 * HEAD, HEAD), h, p, 0, acc[h, :, :, at:at + TILE].reshape(HEAD, TILE))
-            acc[h, :, :, at:at + TILE] = total.reshape(PARTS, ROWS, TILE)
-
-    def out_copy(h):
-        return pltpu.make_async_copy(
-            att.at[h], out_hbm.at[:, pl.ds(pl.multiple_of(h * HEAD, HEAD), HEAD)], out_sem.at[h])
+        held = [acc[h, :, :, p * TILE:(p + 1) * TILE].reshape(HEAD, TILE) for p in range(4)]
+        for p, total in distant(bk[h, 0:5].reshape(5 * HEAD, HEAD), h, 0, held):
+            acc[h, :, :, p * TILE:(p + 1) * TILE] = total.reshape(PARTS, ROWS, TILE)
 
     def far_buckets(i):
         part = i % PARTS
         for n in range(2):
             h = 2 * (i // PARTS) + n
-            for p in range(4):
-                at = p * TILE
-                total = distant(bk[h, 5:8, part].reshape(3 * ROWS, HEAD), h, p, 5, acc[h, part, :, at:at + TILE])
-                att_t[h, part, :, at:at + TILE] = total.astype(BF16)
-
-        @pl.when(part == PARTS - 1)
-        def _():
-            for n in range(2):
-                h = 2 * (i // PARTS) + n
-                att[h] = jnp.transpose(att_t[h].reshape(HEAD, TOK))
-                out_copy(h).start()
+            held = [acc[h, part, :, p * TILE:(p + 1) * TILE] for p in range(4)]
+            for p, total in distant(bk[h, 5:8, part].reshape(3 * ROWS, HEAD), h, 5, held):
+                out[h, part, :, p * TILE:(p + 1) * TILE] = total.astype(BF16)
 
     def when_in(t, at, count):
         return jnp.logical_and(t >= at, t < at + count)
@@ -396,8 +386,6 @@
     def _():
         sent_z(2, sx).wait_send()
     remote(fwd, fwd, f_s.at[0], f_r.at[0, 0], mate).wait_send()
-    for h in range(HEADS):
-        out_copy(h).wait()
 
 
 def layer(queries, keys, values, level_weights, out_weight):
@@ -423,26 +411,24 @@
         pltpu.VMEM((HEADS, 8, PARTS) + item, BF16),
         pltpu.VMEM((HEADS, 3, HEAD, HEAD), BF16),
         pltpu.VMEM((HEADS, PARTS, ROWS, TOK), F32),
-        pltpu.VMEM((HEADS, PARTS, ROWS, TOK), BF16),
-        pltpu.VMEM((HEADS, TOK, HEAD), BF16),
         dma((3, HEADS)), dma((1,)),
         dma((1,)), dma((HEADS // 2,)),
         dma((1,)), dma((ITEMS,)),
         dma((1,)), dma((ITEMS,)),
         dma((3,)), dma((ITEMS, 3)),
         dma((1,)), dma((ITEMS, 3)),
-        dma((HEADS,)),
     ]
     attended = pl.pallas_call(
         kernel,
-        out_shape=jax.ShapeDtypeStruct((TOK, HEADS * HEAD), BF16),
+        out_shape=pltpu.VMEM((HEADS, PARTS, ROWS, TOK), BF16),
         in_specs=[pl.BlockSpec(memory_space=pl.ANY)] * 4,
-        out_specs=pl.BlockSpec(memory_space=pl.ANY),
+        out_specs=pl.BlockSpec(memory_space=pltpu.VMEM),
         scratch_shapes=scratch,
         compiler_params=pltpu.CompilerParams(
             collective_id=0, has_side_effects=True, vmem_limit_bytes=VMEM_MIB << 20),
     )(*[pltpu.with_memory_space_constraint(a, pltpu.HBM) for a in (queries, keys, values, level_weights)])
-    return jnp.dot(attended, out_weight, preferred_element_type=F32).astype(BF16)
+    return lax.dot_general(
+        attended.reshape(HEADS * HEAD, TOK), out_weight, (((0,), (0,)), ((), ())), preferred_element_type=F32).astype(BF16)
 
 
 def solution(mesh):

time: 45.5 us -> 44.4 us (0.976)
  Pallas kernels: 41.8 us -> 40.6 us
    pallas_call x1, Pallas kernels: 41.8 us -> 40.6 us  [layer(): pl.pallas_call(kernel, out_shape=pltpu.VMEM((HEADS, PARTS, ROWS, TOK), BF...]
where the time goes in v2:
time: 44.4 us; the launch traced here: 44.3 us
  Pallas kernels  40.6 us (91%)
  matrix products  3.71 us (8%)
    pallas_call x1, Pallas kernels, layer(): pl.pallas_call(kernel, out_shape=pltpu.VMEM((HEADS, PARTS, ROWS, TOK), BF...  40.6 us
    dot_general x1, matrix products, layer(): lax.dot_general(attended.reshape(HEADS * HEAD, TOK), out_weight, (((0,),...  3.71 us

profile of v2, /device:TPU:1, one launch (start us, length us, event | category | flops | bytes accessed | tf_op | source)
XLA Modules:
  0.0 44.3 jit_solution(10383165022740048125)
XLA Ops:
  0.0 0.0 copy-start
  0.0 40.6 %shard_map.55 = bf16[8,2,64,1024]{3,2,1,0:T(8,128)(2,1)S(1)} custom-call(bf16[1024,1024]{1,0:T(8,128)(2,1)} %q_hbm.1, bf16[1024,1024]{1,0:T(8,128)(2,1)} %k_hbm.1, bf16[1024,1024]{1,0:T(8,128)(2,1)} %v_hbm.1, f32[19,8,1024]{2,1,0:T(8,128)} %lam_hbm.1), custom_call_target="tpu_custom_call" | custom-call | tf_op jit(solution)/shard_map/pallas_call | solution.py:421
  40.6 0.0 copy-done
  40.6 3.7 %convolution_convert_fusion = bf16[1024,1024]{1,0:T(8,128)(2,1)} fusion(bf16[1024,1024]{1,0:T(8,128)(2,1)S(1)} %bitcast.3, bf16[1024,1024]{1,0:T(8,128)(2,1)S(1)} %copy-done), kind=kOutput, calls=%fused_computation | convolution fusion | flops 2148532224 | bytes 6291456 | tf_op jit(solution)/shard_map/dot_general | solution.py:430
Async XLA Ops:
  0.0 40.6 %copy-start = (bf16[1024,1024]{1,0:T(8,128)(2,1)S(1)}, bf16[1024,1024]{1,0:T(8,128)(2,1)}, u32[]{:S(2)}) copy-start(bf16[1024,1024]{1,0:T(8,128)(2,1)} %param.9) | copy-start | bytes 6291460

commit v3 on v2

--- a/solution.py
+++ b/solution.py
@@ -28,7 +28,7 @@
 AT_Z3 = 15
 AT_F2 = 16
 AT_L = 3
-AT_R = 13
+AT_R = 12
 STEPS = ITEMS + AT_F2
 
 
@@ -116,11 +116,11 @@
         return device(to, y, x, c)
 
     def cp_core(h):
-        return remote(st.at[h], ps.at[h], core_s.at[0], core_r.at[h // 2], mate)
-
-    def got_core(k):
-        pair = ps.at[pl.ds(2 * k, 2)]
-        return remote(pair, pair, core_s.at[0], core_r.at[k], mate)
+        return remote(st.at[h], ps.at[h], core_s.at[0], core_r.at[h], mate)
+
+    def take_core(g):
+        cp_core(g).wait_recv()
+        bk[g, 0] = jnp.where(c == 1, ps[g], 0.0).astype(BF16)
 
     def cp_x(i, d):
         return remote(xb.at[i, x], xb.at[i, x], x_s.at[0], x_r.at[i], at_x(d))
@@ -198,10 +198,11 @@
 
         @pl.when(i % PARTS == 0)
         def _():
-            got_core(i // PARTS).wait_recv()
-            for n in range(2):
-                g = 2 * (i // PARTS) + n
-                bk[g, 0] = jnp.where(c == 1, ps[g], 0.0).astype(BF16)
+            take_core(h)
+
+        @pl.when(i % PARTS == PARTS - 1)
+        def _():
+            take_core(2 * (i // PARTS) + 1 - c)
 
         xb[i, x] = st[h, i % PARTS] + ps[h, i % PARTS]
         for d in (2, 1, 3):
@@ -344,7 +345,7 @@
         @pl.when(jnp.logical_and(t % PARTS == 0, t < ITEMS))
         def _():
             for n in range(2):
-                g = 2 * (t // PARTS) + n
+                g = 2 * (t // PARTS) + (1 - c if n == 0 else c)
                 states(g)
                 cp_core(g).start()
 
@@ -359,11 +360,11 @@
         spread(AT_R, near_buckets)
         return carry
 
-    states(0)
-    states(1)
+    states(1 - c)
     pl.semaphore_wait(barrier, len(peers))
-    cp_core(0).start()
-    cp_core(1).start()
+    cp_core(1 - c).start()
+    states(c)
+    cp_core(c).start()
     lax.fori_loop(1, STEPS, step, 0)
 
     remote(st, st, core_s.at[0], core_r.at[0], mate).wait_send()
@@ -412,7 +413,7 @@
         pltpu.VMEM((HEADS, 3, HEAD, HEAD), BF16),
         pltpu.VMEM((HEADS, PARTS, ROWS, TOK), F32),
         dma((3, HEADS)), dma((1,)),
-        dma((1,)), dma((HEADS // 2,)),
+        dma((1,)), dma((HEADS,)),
         dma((1,)), dma((ITEMS,)),
         dma((1,)), dma((ITEMS,)),
         dma((3,)), dma((ITEMS, 3)),

time: 44.4 us -> 44.7 us (level)
  no operation moved by 1% of the time
where the time goes in v3:
time: 44.7 us; the launch traced here: 44.6 us
  Pallas kernels  40.9 us (91%)
  matrix products  3.71 us (8%)
    pallas_call x1, Pallas kernels, layer(): pl.pallas_call(kernel, out_shape=pltpu.VMEM((HEADS, PARTS, ROWS, TOK), BF...  40.9 us
    dot_general x1, matrix products, layer(): lax.dot_general(attended.reshape(HEADS * HEAD, TOK), out_weight, (((0,),...  3.71 us

profile of v3, /device:TPU:1, one launch (start us, length us, event | category | flops | bytes accessed | tf_op | source)
XLA Modules:
  0.0 44.6 jit_solution(2787758974580017567)
XLA Ops:
  0.0 0.0 copy-start
  0.0 40.9 %shard_map.55 = bf16[8,2,64,1024]{3,2,1,0:T(8,128)(2,1)S(1)} custom-call(bf16[1024,1024]{1,0:T(8,128)(2,1)} %q_hbm.1, bf16[1024,1024]{1,0:T(8,128)(2,1)} %k_hbm.1, bf16[1024,1024]{1,0:T(8,128)(2,1)} %v_hbm.1, f32[19,8,1024]{2,1,0:T(8,128)} %lam_hbm.1), custom_call_target="tpu_custom_call" | custom-call | tf_op jit(solution)/shard_map/pallas_call | solution.py:422
  40.9 0.0 copy-done
  40.9 3.7 %convolution_convert_fusion = bf16[1024,1024]{1,0:T(8,128)(2,1)} fusion(bf16[1024,1024]{1,0:T(8,128)(2,1)S(1)} %bitcast.3, bf16[1024,1024]{1,0:T(8,128)(2,1)S(1)} %copy-done), kind=kOutput, calls=%fused_computation | convolution fusion | flops 2148532224 | bytes 6291456 | tf_op jit(solution)/shard_map/dot_general | solution.py:431
Async XLA Ops:
  0.0 40.9 %copy-start = (bf16[1024,1024]{1,0:T(8,128)(2,1)S(1)}, bf16[1024,1024]{1,0:T(8,128)(2,1)}, u32[]{:S(2)}) copy-start(bf16[1024,1024]{1,0:T(8,128)(2,1)} %param.9) | copy-start | bytes 6291460
